TPU v7x, 32 devices: a whole 2x2x4 slice. The times are simulated.
32 devices in a mesh: row: 8 (over y, x, core), col: 4 (over z).
Axes of the slice: x: 2, y: 2, z: 4, core: 2. Of those that a mesh axis runs over, the one named last changes fastest.
Arguments:
- eigvec: float32 [8192, 1024], P('row', 'col'), may hold values from -6 to 6
- refl: float32 [4, 8192, 256], P(None, ('row', 'col')), may hold values from -0.25 to 0.25
- tfac: float32 [4, 4096, 256], P(None, ('row', 'col')), may hold values from -0.375 to 0.375
- sched: int32 [16, 4], P('row'), may hold values from 0 to 3, each once within a row
Outputs:
- result: float32 [8192, 1024], P('row', 'col')
Inputs may be any that keep to these rules, and one draw needn't show every extreme that they name: Each row of sched names every slot 0 to 3 exactly once.
All inputs are finite; a program needn't handle non-finite values.
Results may differ from a plain program's by a relative error of at most 0.0002.
Values sent between devices are 32-bit elements; how exact they have to be, the bound alone decides.
A program may use at most 64 MiB of HBM per device.

v0:
```python
import jax
import jax.numpy as jnp
from jax import lax
from jax.sharding import PartitionSpec as P

B = 512
W = 256


def shifted(block, axis, distance):
    devices = range(lax.axis_size(axis))
    route = [(i - distance, i) for i in devices if i - distance in devices]
    return lax.ppermute(block, axis, route)


def matmul(left, right):
    return jnp.dot(left, right, precision=lax.Precision.HIGHEST, preferred_element_type=jnp.float32)


def apply_block(field, vectors, factor):
    coupling = matmul(vectors.T, field)
    coeffs = matmul(factor, coupling)
    return field - matmul(vectors, coeffs)


def apply_many(field, vectors, factor):
    coupling = jnp.einsum("gbw,gbe->gwe", vectors, field, precision=lax.Precision.HIGHEST)
    coeffs = jnp.einsum("gvw,gwe->gve", factor, coupling, precision=lax.Precision.HIGHEST)
    return field - jnp.einsum("gbw,gwe->gbe", vectors, coeffs, precision=lax.Precision.HIGHEST)


def pick_rows(stored, sched, step_no, col_index, span):
    piece_rows = stored.shape[1]
    local_ids = jnp.arange(piece_rows)
    owners = (col_index * piece_rows + local_ids) // span
    slots = sched[owners, step_no]
    return stored[slots, local_ids]


def on_device(eigvec, refl, tfac, sched):
    total_steps = refl.shape[0]
    local_groups = sched.shape[0]
    evcount = eigvec.shape[1]
    row_index = lax.axis_index("row")
    col_index = lax.axis_index("col")
    last_row = lax.axis_size("row") - 1
    has_block = row_index < last_row
    not_first = row_index > 0
    field = eigvec
    for step_no in range(total_steps):
        picked_v = pick_rows(refl, sched, step_no, col_index, B)
        picked_t = pick_rows(tfac, sched, step_no, col_index, W)
        vectors, factor = (
            lax.all_gather(picked_v, "col", axis=0, tiled=True),
            lax.all_gather(picked_t, "col", axis=0, tiled=True),
        )
        vectors = vectors.reshape(local_groups, B, W)
        factor = factor.reshape(local_groups, W, W)
        if step_no % 2 == 0:
            field = apply_many(field.reshape(local_groups, B, evcount), vectors, factor).reshape(
                local_groups * B, evcount
            )
        else:
            top_rows = field[:W]
            low_rows = field[local_groups * B - W :]
            strad_v = vectors[local_groups - 1]
            strad_t = factor[local_groups - 1]
            inbound = shifted(top_rows, "row", -1)
            joined = jnp.concatenate([low_rows, inbound], axis=0)
            updated = apply_block(joined, strad_v, strad_t)
            new_low = jnp.where(has_block, updated[:W], low_rows)
            returned = shifted(updated[W:], "row", 1)
            new_top = jnp.where(not_first, returned, top_rows)
            middle = field[W : local_groups * B - W].reshape(local_groups - 1, B, evcount)
            middle = apply_many(middle, vectors[: local_groups - 1], factor[: local_groups - 1])
            middle = middle.reshape((local_groups - 1) * B, evcount)
            field = jnp.concatenate([new_top, middle, new_low], axis=0)
    return field


def solution(mesh):
    placed = (
        P("row", "col"),
        P(None, ("row", "col"), None),
        P(None, ("row", "col"), None),
        P("row", None),
    )
    return jax.shard_map(
        on_device, mesh=mesh, in_specs=placed, out_specs=P("row", "col"), check_vma=False
    )
```

profile of v0, /device:TPU:4, one launch (start us, length us, event | category | flops | bytes accessed | tf_op | source)
XLA Modules:
  0.0 173.0 jit_solution(1514608076690900343)
XLA Ops:
  7.3 2.4 %gather_fusion = s32[256]{0:T(256)S(1)} fusion(s32[2,4]{1,0:T(2,128)S(1)} %copy-done.1, s32[256]{0:T(256)S(1)} %bitcast.79), kind=kCustom, calls=%fused_computation | custom fusion | bytes 4096 | tf_op jit(solution)/shard_map/gather | solution.py:36
  9.8 2.7 %gather_fusion.1 = f32[256,256]{1,0:T(8,128)} fusion(f32[4,256,256]{2,1,0:T(8,128)S(1)} %copy-done, s32[256]{0:T(256)S(1)} %bitcast.72), kind=kCustom, calls=%fused_computation.1 | custom fusion | bytes 526336 | tf_op jit(solution)/shard_map/gather | solution.py:37
  12.6 2.4 %gather_fusion.4 = s32[256]{0:T(256)S(1)} fusion(s32[2,4]{1,0:T(2,128)S(1)} %copy-done.1, s32[256]{0:T(256)S(1)} %bitcast.78), kind=kCustom, calls=%fused_computation.4 | custom fusion | bytes 4096 | tf_op jit(solution)/shard_map/gather | solution.py:36
  15.0 2.7 %gather_fusion.5 = f32[256,256]{1,0:T(8,128)} fusion(f32[4,256,256]{2,1,0:T(8,128)S(1)} %copy-done, s32[256]{0:T(256)S(1)} %bitcast.73), kind=kCustom, calls=%fused_computation.5 | custom fusion | bytes 526336 | tf_op jit(solution)/shard_map/gather | solution.py:37
  17.8 2.4 %gather_fusion.8 = s32[256]{0:T(256)S(1)} fusion(s32[2,4]{1,0:T(2,128)S(1)} %copy-done.1, s32[256]{0:T(256)S(1)} %bitcast.77), kind=kCustom, calls=%fused_computation.8 | custom fusion | bytes 4096 | tf_op jit(solution)/shard_map/gather | solution.py:36
  20.3 2.7 %gather_fusion.9 = f32[256,256]{1,0:T(8,128)} fusion(f32[4,256,256]{2,1,0:T(8,128)S(1)} %copy-done, s32[256]{0:T(256)S(1)} %bitcast.74), kind=kCustom, calls=%fused_computation.9 | custom fusion | bytes 526336 | tf_op jit(solution)/shard_map/gather | solution.py:37
  23.1 2.4 %gather_fusion.12 = s32[256]{0:T(256)S(1)} fusion(s32[2,4]{1,0:T(2,128)S(1)} %copy-done.1, s32[256]{0:T(256)S(1)} %bitcast.76), kind=kCustom, calls=%fused_computation.12 | custom fusion | bytes 4096 | tf_op jit(solution)/shard_map/gather | solution.py:36
  25.5 2.7 %gather_fusion.13 = f32[256,256]{1,0:T(8,128)} fusion(f32[4,256,256]{2,1,0:T(8,128)S(1)} %copy-done, s32[256]{0:T(256)S(1)} %bitcast.75), kind=kCustom, calls=%fused_computation.13 | custom fusion | bytes 526336 | tf_op jit(solution)/shard_map/gather | solution.py:37
  28.3 1.5 gather_fusion.2
  31.1 20.3 %all_gather.25 = f32[512,256]{1,0:T(8,128)} all-gather(f32[128,256]{1,0:T(8,128)S(1)} %gather_fusion.3), channel_id=1, replica_groups=mesh['row'=8,'col'=4] {'col'}, dimensions={0}, use_global_device_ids=true | all-gather | bytes 655360 | tf_op jit(solution)/shard_map/all_gather | solution.py:55
  51.4 1.5 gather_fusion.6
  54.2 23.2 %all_gather.27 = f32[512,256]{1,0:T(8,128)} all-gather(f32[128,256]{1,0:T(8,128)S(1)} %gather_fusion.7), channel_id=1, replica_groups=mesh['row'=8,'col'=4] {'col'}, dimensions={0}, use_global_device_ids=true | all-gather | bytes 655360 | tf_op jit(solution)/shard_map/all_gather | solution.py:55
  80.3 16.2 %all_gather.29 = f32[512,256]{1,0:T(8,128)} all-gather(f32[128,256]{1,0:T(8,128)S(1)} %gather_fusion.11), channel_id=1, replica_groups=mesh['row'=8,'col'=4] {'col'}, dimensions={0}, use_global_device_ids=true | all-gather | bytes 655360 | tf_op jit(solution)/shard_map/all_gather | solution.py:55
  99.3 21.3 %all_gather.31 = f32[512,256]{1,0:T(8,128)} all-gather(f32[128,256]{1,0:T(8,128)S(1)} %gather_fusion.15), channel_id=1, replica_groups=mesh['row'=8,'col'=4] {'col'}, dimensions={0}, use_global_device_ids=true | all-gather | bytes 655360 | tf_op jit(solution)/shard_map/all_gather | solution.py:55
  120.6 3.2 %fusion.59 = f32[2,256,256]{2,1,0:T(8,128)S(1)} fusion(f32[2,512,256]{2,1,0:T(8,128)} %bitcast.94, f32[2,512,256]{2,1,0:T(8,128)S(1)} %bitcast.90), kind=kOutput, calls=%fused_computation.115 | convolution fusion | flops 805306368 | bytes 2621440 | tf_op jit(solution)/shard_map/gbw,gbe->gwe/dot_general | solution.py:27
  126.2 2.1 %collective-permute-start = (f32[256,256]{1,0:T(8,128)S(1)}, f32[256,256]{1,0:T(8,128)S(1)}, u32[]{:S(2)}, u32[]{:S(2)}) collective-permute-start(f32[256,256]{1,0:T(8,128)S(1)} %get-tuple-element.12), channel_id=1, source_target_pairs={{4,0},{8,4},{12,8},{16,12},{20,16},{24,20},{28,24},{5,1},{9,5},{13... | collective-permute-start | bytes 786440 | tf_op jit(solution)/shard_map/ppermute | solution.py:13
  128.3 2.1 %fusion.8 = f32[256,256]{1,0:T(8,128)S(1)} fusion(f32[1024,256]{1,0:T(8,128)} %all-gather.7.cloned.1.call-done, f32[1024,256]{1,0:T(8,128)S(1)} %bitcast.85), kind=kOutput, calls=%fused_computation.34 | convolution fusion | flops 402653184 | bytes 1310720 | tf_op jit(solution)/shard_map/gbw,gbe->gwe/dot_general | solution.py:27
  134.1 4.0 %collective-permute-start.1 = (f32[256,256]{1,0:T(8,128)S(1)}, f32[256,256]{1,0:T(8,128)S(1)}, u32[]{:S(2)}, u32[]{:S(2)}) collective-permute-start(f32[256,256]{1,0:T(8,128)S(1)} %slice.116), channel_id=1, source_target_pairs={{0,4},{4,8},{8,12},{12,16},{16,20},{20,24},{24,28},{1,5},{5,9},{9,... | collective-permute-start | bytes 786440 | tf_op jit(solution)/shard_map/ppermute | solution.py:13
  138.7 4.2 %collective-permute-done.1 = f32[256,256]{1,0:T(8,128)S(1)} collective-permute-done((f32[256,256]{1,0:T(8,128)S(1)}, f32[256,256]{1,0:T(8,128)S(1)}, u32[]{:S(2)}, u32[]{:S(2)}) %collective-permute-start.1) | collective-permute-done | bytes 262176 | tf_op jit(solution)/shard_map/ppermute | solution.py:13
  143.1 3.2 %fusion.61 = f32[2,256,256]{2,1,0:T(8,128)S(1)} fusion(f32[2,512,256]{2,1,0:T(8,128)} %bitcast.92, f32[2,512,256]{2,1,0:T(8,128)S(1)} %bitcast.88), kind=kOutput, calls=%fused_computation.117 | convolution fusion | flops 805306368 | bytes 2621440 | tf_op jit(solution)/shard_map/gbw,gbe->gwe/dot_general | solution.py:27
  148.7 2.1 %collective-permute-start.2 = (f32[256,256]{1,0:T(8,128)S(1)}, f32[256,256]{1,0:T(8,128)S(1)}, u32[]{:S(2)}, u32[]{:S(2)}) collective-permute-start(f32[256,256]{1,0:T(8,128)S(1)} %get-tuple-element.8), channel_id=1, source_target_pairs={{4,0},{8,4},{12,8},{16,12},{20,16},{24,20},{28,24},{5,1},{9,5},{13... | collective-permute-start | bytes 786440 | tf_op jit(solution)/shard_map/ppermute | solution.py:13
  152.2 2.1 %fusion.1 = f32[256,256]{1,0:T(8,128)S(1)} fusion(f32[1024,256]{1,0:T(8,128)} %all-gather.11.cloned.1.call-done, f32[1024,256]{1,0:T(8,128)S(1)} %bitcast.81), kind=kOutput, calls=%fused_computation.27 | convolution fusion | flops 402653184 | bytes 1310720 | tf_op jit(solution)/shard_map/gbw,gbe->gwe/dot_general | solution.py:27
  156.8 2.7 %collective-permute-start.3 = (f32[256,256]{1,0:T(8,128)S(1)}, f32[256,256]{1,0:T(8,128)S(1)}, u32[]{:S(2)}, u32[]{:S(2)}) collective-permute-start(f32[256,256]{1,0:T(8,128)S(1)} %slice.125), channel_id=1, source_target_pairs={{0,4},{4,8},{8,12},{12,16},{16,20},{20,24},{24,28},{1,5},{5,9},{9,... | collective-permute-start | bytes 786440 | tf_op jit(solution)/shard_map/ppermute | solution.py:13
  160.1 5.3 %collective-permute-done.3 = f32[256,256]{1,0:T(8,128)S(1)} collective-permute-done((f32[256,256]{1,0:T(8,128)S(1)}, f32[256,256]{1,0:T(8,128)S(1)}, u32[]{:S(2)}, u32[]{:S(2)}) %collective-permute-start.3) | collective-permute-done | bytes 262176 | tf_op jit(solution)/shard_map/ppermute | solution.py:13
  (78 shorter events, 23.9 us)
Async XLA Ops:
  6.5 3.2 %copy-start = (f32[4,256,256]{2,1,0:T(8,128)S(1)}, f32[4,256,256]{2,1,0:T(8,128)}, u32[]{:S(2)}) copy-start(f32[4,256,256]{2,1,0:T(8,128)} %param.5) | copy-start | bytes 3145732
  6.5 114.1 %all-gather.5.cloned.1.call-start = ((), (), s32[]{:S(2)}) async-start(), calls=%async_computation | async-start | bytes 1310720 | tf_op jit(solution)/shard_map/all_gather | solution.py:54
  6.6 0.8 copy-start.1
  12.5 115.7 %all-gather.7.cloned.1.call-start = ((), (), s32[]{:S(2)}) async-start(), calls=%async_computation.1 | async-start | bytes 1310720 | tf_op jit(solution)/shard_map/all_gather | solution.py:54
  17.8 125.3 %all-gather.9.cloned.1.call-start = ((), (), s32[]{:S(2)}) async-start(), calls=%async_computation.2 | async-start | bytes 1310720 | tf_op jit(solution)/shard_map/all_gather | solution.py:54
  23.0 129.2 %all-gather.11.cloned.1.call-start = ((), (), s32[]{:S(2)}) async-start(), calls=%async_computation.3 | async-start | bytes 1310720 | tf_op jit(solution)/shard_map/all_gather | solution.py:54
  28.2 1.6 copy-start.2
  98.0 22.6 %copy-start.3 = (f32[1024,256]{1,0:T(8,128)S(1)}, f32[1024,256]{1,0:T(8,128)}, u32[]{:S(2)}) copy-start(f32[1024,256]{1,0:T(8,128)} %param.4) | copy-start | bytes 3145732
  120.6 3.2 %copy-start.11 = (f32[512,256]{1,0:T(8,128)S(1)}, f32[512,256]{1,0:T(8,128)}, u32[]{:S(2)}) copy-start(f32[512,256]{1,0:T(8,128)} %all_gather.25) | copy-start | bytes 1572868
  123.8 1.2 copy-start.7
  126.2 4.3 %copy-start.10 = (f32[512,256]{1,0:T(8,128)S(1)}, f32[512,256]{1,0:T(8,128)}, u32[]{:S(2)}) copy-start(f32[512,256]{1,0:T(8,128)} %all_gather.27) | copy-start | bytes 1572868
  126.2 5.9 %collective-permute-start = (f32[256,256]{1,0:T(8,128)S(1)}, f32[256,256]{1,0:T(8,128)S(1)}, u32[]{:S(2)}, u32[]{:S(2)}) collective-permute-start(f32[256,256]{1,0:T(8,128)S(1)} %get-tuple-element.12), channel_id=1, source_target_pairs={{4,0},{8,4},{12,8},{16,12},{20,16},{24,20},{28,24},{5,1},{9,5},{13... | collective-permute-start | bytes 786440 | tf_op jit(solution)/shard_map/ppermute | solution.py:13
  128.2 3.8 %copy-start.6 = (f32[1024,256]{1,0:T(8,128)S(1)}, f32[1024,256]{1,0:T(8,128)}, u32[]{:S(2)}) copy-start(f32[1024,256]{1,0:T(8,128)} %all-gather.7.cloned.1.call-done) | copy-start | bytes 3145732
  134.1 8.8 %collective-permute-start.1 = (f32[256,256]{1,0:T(8,128)S(1)}, f32[256,256]{1,0:T(8,128)S(1)}, u32[]{:S(2)}, u32[]{:S(2)}) collective-permute-start(f32[256,256]{1,0:T(8,128)S(1)} %slice.116), channel_id=1, source_target_pairs={{0,4},{4,8},{8,12},{12,16},{16,20},{20,24},{24,28},{1,5},{5,9},{9,... | collective-permute-start | bytes 786440 | tf_op jit(solution)/shard_map/ppermute | solution.py:13
  143.1 3.2 %copy-start.9 = (f32[512,256]{1,0:T(8,128)S(1)}, f32[512,256]{1,0:T(8,128)}, u32[]{:S(2)}) copy-start(f32[512,256]{1,0:T(8,128)} %all_gather.29) | copy-start | bytes 1572868
  146.3 1.2 copy-start.5
  148.6 5.7 %copy-start.8 = (f32[512,256]{1,0:T(8,128)S(1)}, f32[512,256]{1,0:T(8,128)}, u32[]{:S(2)}) copy-start(f32[512,256]{1,0:T(8,128)} %all_gather.31) | copy-start | bytes 1572868
  148.7 6.1 %collective-permute-start.2 = (f32[256,256]{1,0:T(8,128)S(1)}, f32[256,256]{1,0:T(8,128)S(1)}, u32[]{:S(2)}, u32[]{:S(2)}) collective-permute-start(f32[256,256]{1,0:T(8,128)S(1)} %get-tuple-element.8), channel_id=1, source_target_pairs={{4,0},{8,4},{12,8},{16,12},{20,16},{24,20},{28,24},{5,1},{9,5},{13... | collective-permute-start | bytes 786440 | tf_op jit(solution)/shard_map/ppermute | solution.py:13
  152.2 2.6 %copy-start.4 = (f32[1024,256]{1,0:T(8,128)S(1)}, f32[1024,256]{1,0:T(8,128)}, u32[]{:S(2)}) copy-start(f32[1024,256]{1,0:T(8,128)} %all-gather.11.cloned.1.call-done) | copy-start | bytes 3145732
  156.8 8.6 %collective-permute-start.3 = (f32[256,256]{1,0:T(8,128)S(1)}, f32[256,256]{1,0:T(8,128)S(1)}, u32[]{:S(2)}, u32[]{:S(2)}) collective-permute-start(f32[256,256]{1,0:T(8,128)S(1)} %slice.125), channel_id=1, source_target_pairs={{0,4},{4,8},{8,12},{12,16},{16,20},{20,24},{24,28},{1,5},{5,9},{9,... | collective-permute-start | bytes 786440 | tf_op jit(solution)/shard_map/ppermute | solution.py:13
Sparse Core Ops, SparseCore 0:
  12.6 34.7 all-gather.4
  48.9 37.0 all-gather.6
  87.6 36.2 all-gather.8
  125.3 26.8 all-gather.10
where the time goes:
time: 173 us
  blocking collectives  81 us (47%)
  local copies, waits for them, and re-layouts  33.7 us (19%)
  matrix products  20 us (12%)
  between operations  13.7 us (8%)
  waiting for transfers between devices  12.4 us (7%)
  starting transfers between devices  10.9 us (6%)
    all_gather x4, blocking collectives, on_device(): lax.all_gather(picked_t, 'col', axis=0, tiled=True)  81 us
    gather x8, local copies, waits for them, and re-layouts, pick_rows(): return stored[slots, local_ids]  15.9 us
    gather x8, local copies, waits for them, and re-layouts, pick_rows(): slots = sched[owners, step_no]  15.8 us
    ppermute x4, waiting for transfers between devices, shifted(): return lax.ppermute(block, axis, route)  10.8 us
    ppermute x4, starting transfers between devices, shifted(): return lax.ppermute(block, axis, route)  10.8 us
    dot_general x4, matrix products, apply_many(): jnp.einsum('gbw,gbe->gwe', vectors, field, precision=lax.Precision.HIGHEST)  10.6 us
    dot_general x6, matrix products, matmul(): jnp.dot(left, right, precision=lax.Precision.HIGHEST, preferred_element_t...  4 us
  transfers between devices with their start and end apart: 8, of which 4 were waited for; matrix products, arithmetic and copies ran while one was open for 26% of the time, Pallas kernels for 0%

commit v1 on v0

v1 whole, which is shorter than its diff:
```python
import functools

import jax
import jax.numpy as jnp
from jax import lax
from jax.experimental import pallas as pl
from jax.experimental.pallas import tpu as pltpu
from jax.sharding import PartitionSpec as P

B = 512
W = 256
MESH = pl.DeviceIdType.MESH


def split(x):
    high = x.astype(jnp.bfloat16)
    low = (x - high.astype(jnp.float32)).astype(jnp.bfloat16)
    return high, low


def product(left, right, dims):
    def one(a, b):
        return lax.dot_general(a, b, (dims, ((), ())), preferred_element_type=jnp.float32)

    return one(left[0], right[0]) + (one(left[0], right[1]) + one(left[1], right[0]))


def pick_kernel(slots, refl, tfac, packed, hold, in_sem, out_sem):
    steps = packed.shape[0]
    v_rows = refl.shape[1]
    t_rows = tfac.shape[1]
    loads, stores = [], []
    for s in range(steps):
        slot = slots[s]
        loads.append(
            (
                pltpu.make_async_copy(refl.at[slot], hold.at[s, pl.ds(0, v_rows)], in_sem.at[s, 0]),
                pltpu.make_async_copy(tfac.at[slot], hold.at[s, pl.ds(v_rows, t_rows)], in_sem.at[s, 1]),
            )
        )
        stores.append(pltpu.make_async_copy(hold.at[s], packed.at[s], out_sem.at[s]))
    for pair in loads:
        for copy in pair:
            copy.start()
    for pair, store in zip(loads, stores):
        for copy in pair:
            copy.wait()
        store.start()
    for store in stores:
        store.wait()


def main_kernel(n, rows_n, groups, packed, eig, out, field, buf, inb, back, landed, own_sem, eig_sem, out_sem,
                ring_send, ring_recv, up_send, up_recv, down_send, down_recv):
    steps, piece, _ = packed.shape
    v_rows = groups * B // n
    per_group = n // groups
    half = piece // 2
    hops = n // 2
    row = lax.axis_index("row")
    col = lax.axis_index("col")
    right = lax.rem(col + 1, n)
    left = lax.rem(col + n - 1, n)
    has_down = row < rows_n - 1
    has_up = row > 0
    down = jnp.minimum(row + 1, rows_n - 1)
    up = jnp.maximum(row - 1, 0)

    eig_copy = pltpu.make_async_copy(eig, field, eig_sem)
    eig_copy.start()

    barrier = pltpu.get_barrier_semaphore()
    pl.semaphore_signal(barrier, inc=1, device_id=(row, left), device_id_type=MESH)
    pl.semaphore_signal(barrier, inc=1, device_id=(row, right), device_id_type=MESH)

    @pl.when(has_up)
    def _():
        pl.semaphore_signal(barrier, inc=1, device_id=(up, col), device_id_type=MESH)

    @pl.when(has_down)
    def _():
        pl.semaphore_signal(barrier, inc=1, device_id=(down, col), device_id_type=MESH)

    pl.semaphore_wait(barrier, 2 + jnp.minimum(row, 1) + jnp.minimum(rows_n - 1 - row, 1))

    def ring_copy(s, way, hop, part):
        target = right if way == 0 else left
        owner = lax.rem(col + n - hop, n) if way == 0 else lax.rem(col + hop, n)
        span = pl.ds(part * half, half)
        src = packed.at[s, span] if hop == 0 else buf.at[s, owner, span]
        return pltpu.make_async_remote_copy(
            src_ref=src,
            dst_ref=buf.at[s, owner, span],
            send_sem=ring_send.at[s, way, hop, part],
            recv_sem=ring_recv.at[s, way, hop, part],
            device_id=(row, target),
            device_id_type=MESH,
        )

    def parts_of(way, hop):
        order = (0, 1) if way == 0 else (1, 0)
        return order[:1] if hop == hops - 1 else order

    def send_own(s):
        for k in range(len(parts_of(0, 0))):
            for way in (0, 1):
                ring_copy(s, way, 0, parts_of(way, 0)[k]).start()

    def forward(s):
        for hop in range(1, hops):
            for k in range(len(parts_of(0, hop))):
                for way in (0, 1):
                    part = parts_of(way, hop)[k]
                    ring_copy(s, way, hop - 1, part).wait_recv()
                    ring_copy(s, way, hop, part).start()

    def finish(s):
        for hop in range(hops):
            for way in (0, 1):
                done = parts_of(way, hop + 1) if hop + 1 < hops else ()
                for part in parts_of(way, hop):
                    if part not in done:
                        ring_copy(s, way, hop, part).wait_recv()

    def vectors_of(s, g):
        block = buf[s, g * per_group:(g + 1) * per_group, :v_rows]
        return split(block.reshape(B, W))

    def factor_of(s, g):
        block = buf[s, g * per_group:(g + 1) * per_group, v_rows:]
        return split(block.reshape(W, W))

    def coeffs_of(s, g, vectors, rows):
        coupling = product(vectors, split(rows), ((0,), (0,)))
        return split(product(factor_of(s, g), split(coupling), ((1,), (0,))))

    def apply_local(s, g, start):
        vectors = vectors_of(s, g)
        rows = field[start:start + B]
        coeffs = coeffs_of(s, g, vectors, rows)
        field[start:start + B] = rows - product(vectors, coeffs, ((1,), (0,)))

    def up_copy(i):
        return pltpu.make_async_remote_copy(
            src_ref=field.at[pl.ds(0, W)], dst_ref=inb.at[i],
            send_sem=up_send.at[i], recv_sem=up_recv.at[i],
            device_id=(up, col), device_id_type=MESH,
        )

    def down_copy(i):
        return pltpu.make_async_remote_copy(
            src_ref=back.at[i], dst_ref=landed.at[i],
            send_sem=down_send.at[i], recv_sem=down_recv.at[i],
            device_id=(down, col), device_id_type=MESH,
        )

    low = groups * B - W

    send_own(0)
    own = [pltpu.make_async_copy(packed.at[s], buf.at[s, col], own_sem.at[s]) for s in range(steps)]
    for copy in own:
        copy.start()
    eig_copy.wait()
    for s in range(steps):
        forward(s)
        if s + 1 < steps:
            send_own(s + 1)
        own[s].wait()
        finish(s)
        i = s // 2
        if s % 2 == 0:
            for g in range(groups):
                apply_local(s, g, g * B)
                if g == 0 and s + 1 < steps:
                    @pl.when(has_up)
                    def _():
                        up_copy(i).start()
        else:
            @pl.when(has_down)
            def _():
                up_copy(i).wait_recv()
                g = groups - 1
                vectors = vectors_of(s, g)
                rows = jnp.concatenate([field[low:], inb[i]], axis=0)
                coeffs = coeffs_of(s, g, vectors, rows)
                bottom = (vectors[0][W:], vectors[1][W:])
                back[i] = rows[W:] - product(bottom, coeffs, ((1,), (0,)))
                down_copy(i).start()
                top = (vectors[0][:W], vectors[1][:W])
                field[low:] = rows[:W] - product(top, coeffs, ((1,), (0,)))

            for g in range(groups - 1):
                apply_local(s, g, W + g * B)

            @pl.when(has_up)
            def _():
                up_copy(i).wait_send()
                down_copy(i).wait_recv()
                field[:W] = landed[i]

    store = pltpu.make_async_copy(field, out, out_sem)
    store.start()
    for s in range(steps):
        for way in (0, 1):
            for hop in range(hops):
                for part in parts_of(way, hop):
                    ring_copy(s, way, hop, part).wait_send()

    @pl.when(has_down)
    def _():
        for i in range(steps // 2):
            down_copy(i).wait_send()

    store.wait()


def on_device(n, rows_n, eigvec, refl, tfac, sched):
    steps, v_rows, _ = refl.shape
    t_rows = tfac.shape[1]
    groups = sched.shape[0]
    evcount = eigvec.shape[1]
    piece = v_rows + t_rows
    hops = n // 2
    owner = lax.axis_index("col") * v_rows // B
    slots = lax.dynamic_index_in_dim(sched, owner, 0, keepdims=False)
    anywhere = pl.BlockSpec(memory_space=pl.ANY)
    packed = pl.pallas_call(
        pick_kernel,
        out_shape=jax.ShapeDtypeStruct((steps, piece, W), jnp.float32),
        in_specs=[pl.BlockSpec(memory_space=pltpu.SMEM), anywhere, anywhere],
        out_specs=anywhere,
        scratch_shapes=[
            pltpu.VMEM((steps, piece, W), jnp.float32),
            pltpu.SemaphoreType.DMA((steps, 2)),
            pltpu.SemaphoreType.DMA((steps,)),
        ],
        name="pick",
    )(slots, refl, tfac)
    half_steps = steps // 2
    return pl.pallas_call(
        functools.partial(main_kernel, n, rows_n, groups),
        out_shape=jax.ShapeDtypeStruct(eigvec.shape, jnp.float32),
        in_specs=[anywhere, anywhere],
        out_specs=anywhere,
        scratch_shapes=[
            pltpu.VMEM(eigvec.shape, jnp.float32),
            pltpu.VMEM((steps, n, piece, W), jnp.float32),
            pltpu.VMEM((half_steps, W, evcount), jnp.float32),
            pltpu.VMEM((half_steps, W, evcount), jnp.float32),
            pltpu.VMEM((half_steps, W, evcount), jnp.float32),
            pltpu.SemaphoreType.DMA((steps,)),
            pltpu.SemaphoreType.DMA,
            pltpu.SemaphoreType.DMA,
            pltpu.SemaphoreType.DMA((steps, 2, hops, 2)),
            pltpu.SemaphoreType.DMA((steps, 2, hops, 2)),
            pltpu.SemaphoreType.DMA((half_steps,)),
            pltpu.SemaphoreType.DMA((half_steps,)),
            pltpu.SemaphoreType.DMA((half_steps,)),
            pltpu.SemaphoreType.DMA((half_steps,)),
        ],
        compiler_params=pltpu.CompilerParams(
            collective_id=0, has_side_effects=True, vmem_limit_bytes=48 << 20
        ),
        name="sweep",
    )(packed, eigvec)


def solution(mesh):
    placed = (
        P("row", "col"),
        P(None, ("row", "col"), None),
        P(None, ("row", "col"), None),
        P("row", None),
    )
    body = functools.partial(on_device, mesh.shape["col"], mesh.shape["row"])
    return jax.shard_map(body, mesh=mesh, in_specs=placed, out_specs=P("row", "col"), check_vma=False)
```

time: 173 us -> 119 us (0.69)
  the two profiles are of different devices: /device:TPU:4 before, /device:TPU:0 now
where the time goes in v1:
time: 119 us; the launch traced here: 117 us
  Pallas kernels  113 us (95%)
  local copies, waits for them, and re-layouts  3.57 us (3%)
    pallas_call x1, Pallas kernels, on_device(): pl.pallas_call(functools.partial(main_kernel, n, rows_n, groups), out_sha...  110 us
    pallas_call x1, Pallas kernels, on_device(): pl.pallas_call(pick_kernel, out_shape=jax.ShapeDtypeStruct((steps, piece,...  3.08 us
    unnamed x7, local copies, waits for them, and re-layouts  3.06 us

profile of v1, /device:TPU:0, one launch (start us, length us, event | category | flops | bytes accessed | tf_op | source)
XLA Modules:
  0.0 116.7 jit_solution(12235321494012368724)
XLA Ops:
  0.0 0.0 copy-start
  0.0 0.7 copy-done
  0.7 0.5 dynamic-slice_bitcast_fusion.slots
  1.2 0.0 copy-start.2
  1.2 3.1 %pick.1.packed = f32[4,384,256]{2,1,0:T(8,128)} custom-call(s32[4]{0:T(128)} %dynamic-slice_bitcast_fusion.slots, f32[4,256,256]{2,1,0:T(8,128)} %refl.1, f32[4,128,256]{2,1,0:T(8,128)} %tfac.1), custom_call_target="tpu_custom_call" | custom-call | tf_op jit(solution)/shard_map/pick/pallas_call | solution.py:227
  4.3 0.0 copy-done.2
  4.3 0.0 copy-start.1
  4.3 1.4 %copy-done.1 = f32[4,384,256]{2,1,0:T(8,128)S(1)} copy-done((f32[4,384,256]{2,1,0:T(8,128)S(1)}, f32[4,384,256]{2,1,0:T(8,128)}, u32[]{:S(2)}) %copy-start.1) | copy-done | bytes 1572888
  5.7 110.0 %sweep.1 = f32[1024,256]{1,0:T(8,128)S(1)} custom-call(f32[4,384,256]{2,1,0:T(8,128)S(1)} %copy-done.1, f32[1024,256]{1,0:T(8,128)S(1)} %copy-done.2), custom_call_target="tpu_custom_call" | custom-call | tf_op jit(solution)/shard_map/sweep/pallas_call | solution.py:240
  115.7 1.0 copy.6
Async XLA Ops:
  0.0 0.7 copy-start
  1.2 3.1 %copy-start.2 = (f32[1024,256]{1,0:T(8,128)S(1)}, f32[1024,256]{1,0:T(8,128)}, u32[]{:S(2)}) copy-start(f32[1024,256]{1,0:T(8,128)} %eig.1) | copy-start | bytes 3145732
  4.3 1.4 %copy-start.1 = (f32[4,384,256]{2,1,0:T(8,128)S(1)}, f32[4,384,256]{2,1,0:T(8,128)}, u32[]{:S(2)}) copy-start(f32[4,384,256]{2,1,0:T(8,128)} %pick.1.packed) | copy-start | bytes 4718596

commit v2 on v1

--- a/solution.py
+++ b/solution.py
@@ -214,6 +214,248 @@
     store.wait()
 
 
+def line_kernel(rows_n, packed, eig, out, field, buf, inb, back, landed, own_sem, eig_sem, out_sem,
+                feed_send, feed_recv, cols_send, cols_recv, cross_send, cross_recv,
+                up_send, up_recv, down_send, down_recv, res_send, res_recv):
+    steps, piece, _ = packed.shape
+    v_rows = B // 2
+    low = B + W
+    last = steps - 1
+    row = lax.axis_index("row")
+    col = lax.axis_index("col")
+    inner = (col == 1) | (col == 2)
+    partner = col + 1 - 2 * lax.rem(col, 2)
+    other = 3 - col
+    has_down = row < rows_n - 1
+    has_up = row > 0
+    down = jnp.minimum(row + 1, rows_n - 1)
+    up = jnp.maximum(row - 1, 0)
+
+    def remote(src, dst, send, recv, target):
+        return pltpu.make_async_remote_copy(
+            src_ref=src, dst_ref=dst, send_sem=send, recv_sem=recv,
+            device_id=target, device_id_type=MESH,
+        )
+
+    def greet(target):
+        pl.semaphore_signal(barrier, inc=1, device_id=target, device_id_type=MESH)
+
+    barrier = pltpu.get_barrier_semaphore()
+    some_up = jnp.minimum(row, 1)
+    some_down = jnp.minimum(rows_n - 1 - row, 1)
+    greet((row, partner))
+
+    @pl.when(inner)
+    def _():
+        greet((row, other))
+
+        @pl.when(has_up)
+        def _():
+            greet((up, col))
+
+        @pl.when(has_down)
+        def _():
+            greet((down, col))
+            greet((down, partner))
+
+    @pl.when(jnp.logical_not(inner) & has_up)
+    def _():
+        greet((up, partner))
+
+    @pl.when(inner)
+    def _():
+        pl.semaphore_wait(barrier, 2 + some_up + 2 * some_down)
+
+    @pl.when(jnp.logical_not(inner))
+    def _():
+        pl.semaphore_wait(barrier, 1 + some_up)
+
+    def feed(s, owner):
+        return remote(packed.at[s], buf.at[s, owner], feed_send.at[s], feed_recv.at[s], (row, partner))
+
+    columns = remote(eig, field.at[1], cols_send, cols_recv, (row, partner))
+
+    def cross(s, k):
+        owner = col if k == 0 else partner
+        src = packed.at[s] if k == 0 else buf.at[s, owner]
+        return remote(src, buf.at[s, owner], cross_send.at[s, k], cross_recv.at[s, k], (row, other))
+
+    def result(part, src, target_row):
+        span = (pl.ds(0, W), pl.ds(W, B), pl.ds(low, W))[part]
+        return remote(src, out.at[span], res_send.at[part], res_recv.at[part], (target_row, partner))
+
+    @pl.when(jnp.logical_not(inner))
+    def _():
+        feed(0, col).start()
+        feed(1, col).start()
+        columns.start()
+        for s in range(2, steps):
+            feed(s, col).start()
+        for s in range(steps):
+            feed(s, col).wait_send()
+        columns.wait_send()
+        for part in range(3):
+            rows = (W, B, W)[part]
+            result(part, field.at[0, pl.ds(0, rows)], row).wait_recv()
+
+    def vectors_of(s, g):
+        return split(buf[s, 2 * g:2 * g + 2, :v_rows].reshape(B, W))
+
+    def factor_of(s, g):
+        return split(buf[s, 2 * g:2 * g + 2, v_rows:].reshape(W, W))
+
+    def coeffs_of(vectors, factor, rows):
+        coupling = product(vectors, split(rows), ((0,), (0,)))
+        return split(product(factor, split(coupling), ((1,), (0,))))
+
+    def apply_local(s, g, z, start):
+        vectors = vectors_of(s, g)
+        rows = field[z, start:start + B]
+        coeffs = coeffs_of(vectors, factor_of(s, g), rows)
+        field[z, start:start + B] = rows - product(vectors, coeffs, ((1,), (0,)))
+
+    def up_copy(i, z):
+        return remote(field.at[z, pl.ds(0, W)], inb.at[i, z], up_send.at[i, z], up_recv.at[i, z], (up, col))
+
+    def down_copy(i, z):
+        return remote(back.at[i, z], landed.at[i, z], down_send.at[i, z], down_recv.at[i, z], (down, col))
+
+    def even(s, z):
+        for g in range(2):
+            apply_local(s, g, z, g * B)
+            if g == 0:
+                @pl.when(has_up)
+                def _():
+                    up_copy(s // 2, z).start()
+
+    def straddle(s, z, send):
+        i = s // 2
+
+        @pl.when(has_down)
+        def _():
+            up_copy(i, z).wait_recv()
+            vectors = vectors_of(s, 1)
+            rows = jnp.concatenate([field[z, low:], inb[i, z]], axis=0)
+            coeffs = coeffs_of(vectors, factor_of(s, 1), rows)
+            bottom = (vectors[0][W:], vectors[1][W:])
+            back[i, z] = rows[W:] - product(bottom, coeffs, ((1,), (0,)))
+            send()
+            top = (vectors[0][:W], vectors[1][:W])
+            field[z, low:] = rows[:W] - product(top, coeffs, ((1,), (0,)))
+
+    def settle(s, z):
+        @pl.when(has_up)
+        def _():
+            up_copy(s // 2, z).wait_send()
+            down_copy(s // 2, z).wait_recv()
+            field[z, :W] = landed[s // 2, z]
+
+    @pl.when(inner)
+    def _():
+        eig_copy = pltpu.make_async_copy(eig, field.at[0], eig_sem)
+        own = [pltpu.make_async_copy(packed.at[s], buf.at[s, col], own_sem.at[s]) for s in range(steps)]
+
+        def near(s):
+            own[s].wait()
+
+        def far(s):
+            for k in range(2):
+                cross(s, k).wait_recv()
+
+        def relay(s):
+            feed(s, partner).wait_recv()
+            cross(s, 1).start()
+
+        cross(0, 0).start()
+        eig_copy.start()
+        for copy in own:
+            copy.start()
+        cross(1, 0).start()
+        relay(0)
+        eig_copy.wait()
+        relay(1)
+        for s in range(2, steps):
+            cross(s, 0).start()
+        near(0)
+        far(0)
+        even(0, 0)
+        near(1)
+        far(1)
+        straddle(1, 0, lambda: down_copy(0, 0).start())
+        apply_local(1, 0, 0, W)
+        settle(1, 0)
+        columns.wait_recv()
+        even(0, 1)
+        straddle(1, 1, lambda: down_copy(0, 1).start())
+        apply_local(1, 0, 1, W)
+        relay(2)
+        settle(1, 1)
+        near(2)
+        far(2)
+        even(2, 1)
+        relay(3)
+        even(2, 0)
+        near(3)
+
+        def last_straddle():
+            i = last // 2
+            straddle(last, 1, lambda: result(0, back.at[i, 1], down).start())
+            result(2, field.at[1, pl.ds(low, W)], row).start()
+            straddle(last, 0, lambda: down_copy(i, 0).start())
+
+            @pl.when(has_up)
+            def _():
+                up_copy(i, 1).wait_send()
+                up_copy(i, 0).wait_send()
+
+            @pl.when(jnp.logical_not(has_up))
+            def _():
+                result(0, field.at[1, pl.ds(0, W)], row).start()
+
+        def last_local():
+            apply_local(last, 0, 1, W)
+            result(1, field.at[1, pl.ds(W, B)], row).start()
+            apply_local(last, 0, 0, W)
+
+        @pl.when(col == 1)
+        def _():
+            last_local()
+            far(last)
+            last_straddle()
+
+        @pl.when(col == 2)
+        def _():
+            last_straddle()
+            far(last)
+            last_local()
+
+        @pl.when(has_up)
+        def _():
+            down_copy(last // 2, 0).wait_recv()
+            field[0, :W] = landed[last // 2, 0]
+
+        store = pltpu.make_async_copy(field.at[0], out, out_sem)
+        store.start()
+        for s in range(steps):
+            for k in range(2):
+                cross(s, k).wait_send()
+
+        @pl.when(has_down)
+        def _():
+            down_copy(0, 0).wait_send()
+            down_copy(0, 1).wait_send()
+            down_copy(last // 2, 0).wait_send()
+            result(0, back.at[last // 2, 1], down).wait_send()
+
+        @pl.when(jnp.logical_not(has_up))
+        def _():
+            result(0, field.at[1, pl.ds(0, W)], row).wait_send()
+
+        result(1, field.at[1, pl.ds(W, B)], row).wait_send()
+        result(2, field.at[1, pl.ds(low, W)], row).wait_send()
+        store.wait()
+
+
 def on_device(n, rows_n, eigvec, refl, tfac, sched):
     steps, v_rows, _ = refl.shape
     t_rows = tfac.shape[1]
@@ -237,6 +479,40 @@
         name="pick",
     )(slots, refl, tfac)
     half_steps = steps // 2
+    if n == 4 and groups == 2 and steps == 4:
+        two = (half_steps, 2)
+        return pl.pallas_call(
+            functools.partial(line_kernel, rows_n),
+            out_shape=jax.ShapeDtypeStruct(eigvec.shape, jnp.float32),
+            in_specs=[anywhere, anywhere],
+            out_specs=anywhere,
+            scratch_shapes=[
+                pltpu.VMEM((2, *eigvec.shape), jnp.float32),
+                pltpu.VMEM((steps, n, piece, W), jnp.float32),
+                pltpu.VMEM((*two, W, evcount), jnp.float32),
+                pltpu.VMEM((*two, W, evcount), jnp.float32),
+                pltpu.VMEM((*two, W, evcount), jnp.float32),
+                pltpu.SemaphoreType.DMA((steps,)),
+                pltpu.SemaphoreType.DMA,
+                pltpu.SemaphoreType.DMA,
+                pltpu.SemaphoreType.DMA((steps,)),
+                pltpu.SemaphoreType.DMA((steps,)),
+                pltpu.SemaphoreType.DMA,
+                pltpu.SemaphoreType.DMA,
+                pltpu.SemaphoreType.DMA((steps, 2)),
+                pltpu.SemaphoreType.DMA((steps, 2)),
+                pltpu.SemaphoreType.DMA(two),
+                pltpu.SemaphoreType.DMA(two),
+                pltpu.SemaphoreType.DMA(two),
+                pltpu.SemaphoreType.DMA(two),
+                pltpu.SemaphoreType.DMA((3,)),
+                pltpu.SemaphoreType.DMA((3,)),
+            ],
+            compiler_params=pltpu.CompilerParams(
+                collective_id=0, has_side_effects=True, vmem_limit_bytes=48 << 20
+            ),
+            name="sweep",
+        )(packed, eigvec)
     return pl.pallas_call(
         functools.partial(main_kernel, n, rows_n, groups),
         out_shape=jax.ShapeDtypeStruct(eigvec.shape, jnp.float32),

time: 119 us -> 107 us (0.90); the launches traced: 117 us -> 107 us
  Pallas kernels: 113 us -> 103 us
    pallas_call x1, Pallas kernels: 110 us -> 100 us  [on_device(): pl.pallas_call(functools.partial(line_kernel, rows_n), out_shape=jax.Shap...]
where the time goes in v2:
time: 107 us
  Pallas kernels  103 us (96%)
  local copies, waits for them, and re-layouts  3.57 us (3%)
    pallas_call x1, Pallas kernels, on_device(): pl.pallas_call(functools.partial(line_kernel, rows_n), out_shape=jax.Shap...  100 us
    pallas_call x1, Pallas kernels, on_device(): pl.pallas_call(pick_kernel, out_shape=jax.ShapeDtypeStruct((steps, piece,...  3.08 us
    unnamed x7, local copies, waits for them, and re-layouts  3.06 us

profile of v2, /device:TPU:0, one launch (start us, length us, event | category | flops | bytes accessed | tf_op | source)
XLA Modules:
  0.0 106.9 jit_solution(11210502644151801704)
XLA Ops:
  0.0 0.0 copy-start
  0.0 0.7 copy-done
  0.7 0.5 dynamic-slice_bitcast_fusion.slots
  1.2 0.0 copy-start.2
  1.2 3.1 %pick.1.packed = f32[4,384,256]{2,1,0:T(8,128)} custom-call(s32[4]{0:T(128)} %dynamic-slice_bitcast_fusion.slots, f32[4,256,256]{2,1,0:T(8,128)} %refl.1, f32[4,128,256]{2,1,0:T(8,128)} %tfac.1), custom_call_target="tpu_custom_call" | custom-call | tf_op jit(solution)/shard_map/pick/pallas_call | solution.py:469
  4.3 0.0 copy-done.2
  4.3 0.0 copy-start.1
  4.3 1.4 %copy-done.1 = f32[4,384,256]{2,1,0:T(8,128)S(1)} copy-done((f32[4,384,256]{2,1,0:T(8,128)S(1)}, f32[4,384,256]{2,1,0:T(8,128)}, u32[]{:S(2)}) %copy-start.1) | copy-done | bytes 1572888
  5.7 100.2 %sweep.1 = f32[1024,256]{1,0:T(8,128)S(1)} custom-call(f32[4,384,256]{2,1,0:T(8,128)S(1)} %copy-done.1, f32[1024,256]{1,0:T(8,128)S(1)} %copy-done.2), custom_call_target="tpu_custom_call" | custom-call | tf_op jit(solution)/shard_map/sweep/pallas_call | solution.py:484
  105.9 1.0 copy.6
Async XLA Ops:
  0.0 0.7 copy-start
  1.2 3.1 %copy-start.2 = (f32[1024,256]{1,0:T(8,128)S(1)}, f32[1024,256]{1,0:T(8,128)}, u32[]{:S(2)}) copy-start(f32[1024,256]{1,0:T(8,128)} %eig.1) | copy-start | bytes 3145732
  4.3 1.4 %copy-start.1 = (f32[4,384,256]{2,1,0:T(8,128)S(1)}, f32[4,384,256]{2,1,0:T(8,128)}, u32[]{:S(2)}) copy-start(f32[4,384,256]{2,1,0:T(8,128)} %pick.1.packed) | copy-start | bytes 4718596

commit v3 on v2

--- a/solution.py
+++ b/solution.py
@@ -273,7 +273,9 @@
     def feed(s, owner):
         return remote(packed.at[s], buf.at[s, owner], feed_send.at[s], feed_recv.at[s], (row, partner))
 
-    columns = remote(eig, field.at[1], cols_send, cols_recv, (row, partner))
+    def columns(g):
+        span = pl.ds(g * B, B)
+        return remote(eig.at[span], field.at[1, span], cols_send.at[g], cols_recv.at[g], (row, partner))
 
     def cross(s, k):
         owner = col if k == 0 else partner
@@ -287,13 +289,15 @@
     @pl.when(jnp.logical_not(inner))
     def _():
         feed(0, col).start()
+        columns(0).start()
         feed(1, col).start()
-        columns.start()
+        columns(1).start()
         for s in range(2, steps):
             feed(s, col).start()
         for s in range(steps):
             feed(s, col).wait_send()
-        columns.wait_send()
+        columns(0).wait_send()
+        columns(1).wait_send()
         for part in range(3):
             rows = (W, B, W)[part]
             result(part, field.at[0, pl.ds(0, rows)], row).wait_recv()
@@ -372,28 +376,35 @@
             copy.start()
         cross(1, 0).start()
         relay(0)
+        cross(2, 0).start()
         eig_copy.wait()
-        relay(1)
-        for s in range(2, steps):
-            cross(s, 0).start()
         near(0)
         far(0)
         even(0, 0)
+        columns(0).wait_recv()
+        apply_local(0, 0, 1, 0)
+
+        @pl.when(has_up)
+        def _():
+            up_copy(0, 1).start()
+
+        relay(1)
+        cross(3, 0).start()
+        columns(1).wait_recv()
+        apply_local(0, 1, 1, B)
         near(1)
         far(1)
-        straddle(1, 0, lambda: down_copy(0, 0).start())
-        apply_local(1, 0, 0, W)
-        settle(1, 0)
-        columns.wait_recv()
-        even(0, 1)
         straddle(1, 1, lambda: down_copy(0, 1).start())
         apply_local(1, 0, 1, W)
         relay(2)
+        straddle(1, 0, lambda: down_copy(0, 0).start())
+        apply_local(1, 0, 0, W)
         settle(1, 1)
+        settle(1, 0)
+        relay(3)
         near(2)
         far(2)
         even(2, 1)
-        relay(3)
         even(2, 0)
         near(3)
 
@@ -497,8 +508,8 @@
                 pltpu.SemaphoreType.DMA,
                 pltpu.SemaphoreType.DMA((steps,)),
                 pltpu.SemaphoreType.DMA((steps,)),
-                pltpu.SemaphoreType.DMA,
-                pltpu.SemaphoreType.DMA,
+                pltpu.SemaphoreType.DMA((2,)),
+                pltpu.SemaphoreType.DMA((2,)),
                 pltpu.SemaphoreType.DMA((steps, 2)),
                 pltpu.SemaphoreType.DMA((steps, 2)),
                 pltpu.SemaphoreType.DMA(two),

time: 107 us -> 107 us (level)
  no operation moved by 1% of the time
where the time goes in v3:
time: 107 us
  Pallas kernels  103 us (96%)
  local copies, waits for them, and re-layouts  3.57 us (3%)
    pallas_call x1, Pallas kernels, on_device(): pl.pallas_call(functools.partial(line_kernel, rows_n), out_shape=jax.Shap...  100 us
    pallas_call x1, Pallas kernels, on_device(): pl.pallas_call(pick_kernel, out_shape=jax.ShapeDtypeStruct((steps, piece,...  3.08 us
    unnamed x7, local copies, waits for them, and re-layouts  3.06 us

profile of v3, /device:TPU:0, one launch (start us, length us, event | category | flops | bytes accessed | tf_op | source)
XLA Modules:
  0.0 106.7 jit_solution(9924363816613617511)
XLA Ops:
  0.0 0.0 copy-start
  0.0 0.7 copy-done
  0.7 0.5 dynamic-slice_bitcast_fusion.slots
  1.2 0.0 copy-start.2
  1.2 3.1 %pick.1.packed = f32[4,384,256]{2,1,0:T(8,128)} custom-call(s32[4]{0:T(128)} %dynamic-slice_bitcast_fusion.slots, f32[4,256,256]{2,1,0:T(8,128)} %refl.1, f32[4,128,256]{2,1,0:T(8,128)} %tfac.1), custom_call_target="tpu_custom_call" | custom-call | tf_op jit(solution)/shard_map/pick/pallas_call | solution.py:480
  4.3 0.0 copy-done.2
  4.3 0.0 copy-start.1
  4.3 1.4 %copy-done.1 = f32[4,384,256]{2,1,0:T(8,128)S(1)} copy-done((f32[4,384,256]{2,1,0:T(8,128)S(1)}, f32[4,384,256]{2,1,0:T(8,128)}, u32[]{:S(2)}) %copy-start.1) | copy-done | bytes 1572888
  5.7 100.1 %sweep.1 = f32[1024,256]{1,0:T(8,128)S(1)} custom-call(f32[4,384,256]{2,1,0:T(8,128)S(1)} %copy-done.1, f32[1024,256]{1,0:T(8,128)S(1)} %copy-done.2), custom_call_target="tpu_custom_call" | custom-call | tf_op jit(solution)/shard_map/sweep/pallas_call | solution.py:495
  105.8 1.0 copy.6
Async XLA Ops:
  0.0 0.7 copy-start
  1.2 3.1 %copy-start.2 = (f32[1024,256]{1,0:T(8,128)S(1)}, f32[1024,256]{1,0:T(8,128)}, u32[]{:S(2)}) copy-start(f32[1024,256]{1,0:T(8,128)} %eig.1) | copy-start | bytes 3145732
  4.3 1.4 %copy-start.1 = (f32[4,384,256]{2,1,0:T(8,128)S(1)}, f32[4,384,256]{2,1,0:T(8,128)}, u32[]{:S(2)}) copy-start(f32[4,384,256]{2,1,0:T(8,128)} %pick.1.packed) | copy-start | bytes 4718596

commit v4 on v3

--- a/solution.py
+++ b/solution.py
@@ -291,9 +291,9 @@
         feed(0, col).start()
         columns(0).start()
         feed(1, col).start()
+        feed(2, col).start()
         columns(1).start()
-        for s in range(2, steps):
-            feed(s, col).start()
+        feed(3, col).start()
         for s in range(steps):
             feed(s, col).wait_send()
         columns(0).wait_send()
@@ -389,22 +389,31 @@
             up_copy(0, 1).start()
 
         relay(1)
+        relay(2)
         cross(3, 0).start()
+        near(1)
+        far(1)
+        straddle(1, 0, lambda: down_copy(0, 0).start())
+        apply_local(1, 0, 0, W)
         columns(1).wait_recv()
         apply_local(0, 1, 1, B)
-        near(1)
-        far(1)
         straddle(1, 1, lambda: down_copy(0, 1).start())
         apply_local(1, 0, 1, W)
-        relay(2)
-        straddle(1, 0, lambda: down_copy(0, 0).start())
-        apply_local(1, 0, 0, W)
+        settle(1, 0)
         settle(1, 1)
-        settle(1, 0)
-        relay(3)
+
+        @pl.when(lax.rem(row, 2) == 0)
+        def _():
+            relay(3)
+
         near(2)
         far(2)
         even(2, 1)
+
+        @pl.when(lax.rem(row, 2) == 1)
+        def _():
+            relay(3)
+
         even(2, 0)
         near(3)
 

time: 107 us -> 101 us (0.944); the launches traced: 107 us -> 99.3 us
  Pallas kernels: 103 us -> 95.7 us
    pallas_call x1, Pallas kernels: 100 us -> 92.6 us  [on_device(): pl.pallas_call(functools.partial(line_kernel, rows_n), out_shape=jax.Shap...]
where the time goes in v4:
time: 101 us; the launch traced here: 99.3 us
  Pallas kernels  95.7 us (95%)
  local copies, waits for them, and re-layouts  3.57 us (4%)
    pallas_call x1, Pallas kernels, on_device(): pl.pallas_call(functools.partial(line_kernel, rows_n), out_shape=jax.Shap...  92.6 us
    pallas_call x1, Pallas kernels, on_device(): pl.pallas_call(pick_kernel, out_shape=jax.ShapeDtypeStruct((steps, piece,...  3.08 us
    unnamed x7, local copies, waits for them, and re-layouts  3.06 us

profile of v4, /device:TPU:0, one launch (start us, length us, event | category | flops | bytes accessed | tf_op | source)
XLA Modules:
  0.0 99.3 jit_solution(13317969851282741557)
XLA Ops:
  0.0 0.0 copy-start
  0.0 0.7 copy-done
  0.7 0.5 dynamic-slice_bitcast_fusion.slots
  1.2 0.0 copy-start.2
  1.2 3.1 %pick.1.packed = f32[4,384,256]{2,1,0:T(8,128)} custom-call(s32[4]{0:T(128)} %dynamic-slice_bitcast_fusion.slots, f32[4,256,256]{2,1,0:T(8,128)} %refl.1, f32[4,128,256]{2,1,0:T(8,128)} %tfac.1), custom_call_target="tpu_custom_call" | custom-call | tf_op jit(solution)/shard_map/pick/pallas_call | solution.py:489
  4.3 0.0 copy-done.2
  4.3 0.0 copy-start.1
  4.3 1.4 %copy-done.1 = f32[4,384,256]{2,1,0:T(8,128)S(1)} copy-done((f32[4,384,256]{2,1,0:T(8,128)S(1)}, f32[4,384,256]{2,1,0:T(8,128)}, u32[]{:S(2)}) %copy-start.1) | copy-done | bytes 1572888
  5.7 92.6 %sweep.1 = f32[1024,256]{1,0:T(8,128)S(1)} custom-call(f32[4,384,256]{2,1,0:T(8,128)S(1)} %copy-done.1, f32[1024,256]{1,0:T(8,128)S(1)} %copy-done.2), custom_call_target="tpu_custom_call" | custom-call | tf_op jit(solution)/shard_map/sweep/pallas_call | solution.py:504
  98.3 1.0 copy.6
Async XLA Ops:
  0.0 0.7 copy-start
  1.2 3.1 %copy-start.2 = (f32[1024,256]{1,0:T(8,128)S(1)}, f32[1024,256]{1,0:T(8,128)}, u32[]{:S(2)}) copy-start(f32[1024,256]{1,0:T(8,128)} %eig.1) | copy-start | bytes 3145732
  4.3 1.4 %copy-start.1 = (f32[4,384,256]{2,1,0:T(8,128)S(1)}, f32[4,384,256]{2,1,0:T(8,128)}, u32[]{:S(2)}) copy-start(f32[4,384,256]{2,1,0:T(8,128)} %pick.1.packed) | copy-start | bytes 4718596
